TPU v7x, 256 devices: a whole 4x4x8 slice. The times are simulated.
256 devices in a mesh: pb: 16 (over x, z_hi), sa: 16 (over z_lo, y, core).
Axes of the slice: x: 4, y: 4, z: 8 (z_hi: 4, z_lo: 2; z = z_hi * 2 + z_lo), core: 2. Of those that a mesh axis runs over, the one named last changes fastest.
Arguments:
- question_states: bfloat16 [16, 16, 256, 768], P('pb', 'sa'), may hold values from -16 to 16
- question_ids: int32 [16, 16, 256], P('pb'), may hold values from 0 to 30521, as said below
- q_inner_weight: bfloat16 [768, 3072], P(None, 'sa'), may hold values from -0.21875 to 0.21875
- q_outer_weight: bfloat16 [3072, 768], P('sa'), may hold values from -0.109375 to 0.109375
- q_norm_gain: float32 [768], replicated, may hold values from 0.1 to 1.9
- sql_states: bfloat16 [16, 16, 256, 768], P('sa', 'pb'), may hold values from -16 to 16
- sql_ids: int32 [16, 16, 256], P('sa'), may hold values from 0 to 32099, as said below
- s_inner_weight: bfloat16 [768, 3072], P(None, 'pb'), may hold values from -0.21875 to 0.21875
- s_outer_weight: bfloat16 [3072, 768], P('pb'), may hold values from -0.109375 to 0.109375
- s_norm_gain: float32 [768], replicated, may hold values from 0.1 to 1.9
- positive_column: int32 [256], P('pb'), may hold values from 0 to 255, each once
Outputs:
- loss: float32 [], replicated
- q_inner_grad: float32 [768, 3072], P(None, 'sa')
- q_outer_grad: float32 [3072, 768], P('sa')
- q_gain_grad: float32 [768], replicated
- s_inner_grad: float32 [768, 3072], P(None, 'pb')
- s_outer_grad: float32 [3072, 768], P('pb')
- s_gain_grad: float32 [768], replicated
Inputs may be any that keep to these rules, and one draw needn't show every extreme that they name: `question_ids`: each sequence is a run of nonzero ids followed by padding zeros, the run 3 * 64 long or longer. `sql_ids`: each sequence is a run of nonzero ids followed by padding zeros, the run 3 * 64 long or longer.
All inputs are finite; a program needn't handle non-finite values.
Results may differ from a plain program's by a relative error of at most 0.0051.
Values may be sent and summed in bfloat16 or wider, within the bound.
A program may use at most 128 MiB of HBM per device.

v0:
```python
import math
import jax
import jax.numpy as jnp
from jax import lax
from jax.sharding import PartitionSpec as P

D = 768
HIGH = lax.Precision.HIGHEST


def apply_rms_norm(input_float, norm_gain_vector, root_mean_square):
    if root_mean_square:
        input_normalized = input_float * lax.rsqrt(
            jnp.mean(input_float * input_float, axis=-1, keepdims=True) + 1e-06
        )
    else:
        mean_removed = input_float - jnp.mean(input_float, axis=-1, keepdims=True)
        input_normalized = mean_removed * lax.rsqrt(
            jnp.mean(mean_removed * mean_removed, axis=-1, keepdims=True) + 1e-05
        )
    return (input_normalized, (input_normalized * norm_gain_vector).astype(jnp.bfloat16))


def gelu_value(v):
    return 0.5 * v * (1.0 + lax.erf(v / math.sqrt(2.0)))


def gelu_slope(v):
    return 0.5 * (1.0 + lax.erf(v / math.sqrt(2.0))) + v * jnp.exp(-0.5 * v * v) / math.sqrt(
        2.0 * math.pi
    )


def pool_weights(ids):
    mask = (ids > 0).astype(jnp.float32)
    return mask / jnp.sum(mask, axis=-1, keepdims=True)


def tower_forward(tokens, ids, inner, gain, root_mean_square):
    count, length, width = tokens.shape
    input_float = tokens.astype(jnp.float32).reshape(count * length, width)
    input_normalized, normalized_rows = apply_rms_norm(input_float, gain, root_mean_square)
    pre = jnp.dot(normalized_rows, inner, preferred_element_type=jnp.float32)
    weights = pool_weights(ids)
    hidden = gelu_value(pre).reshape(count, length, -1)
    pooled = jnp.einsum("nt,ntf->nf", weights, hidden, precision=HIGH)
    resid = jnp.einsum(
        "nt,ntd->nd", weights, input_float.reshape(count, length, width), precision=HIGH
    )
    return (input_normalized, normalized_rows, pre, weights, pooled, resid)


def tower_backward(input_normalized, normalized_rows, pre, weights, inner, hidden_grad):
    count, length = weights.shape
    slope = gelu_slope(pre).reshape(count, length, -1)
    dpre = (
        (weights[:, :, None] * hidden_grad[:, None, :] * slope)
        .reshape(count * length, -1)
        .astype(jnp.bfloat16)
    )
    inner_part = lax.dot_general(
        normalized_rows, dpre, (((0,), (0,)), ((), ())), preferred_element_type=jnp.float32
    )
    normalized_grad = lax.dot_general(
        dpre, inner, (((1,), (1,)), ((), ())), preferred_element_type=jnp.float32
    )
    return (inner_part, jnp.sum(input_normalized * normalized_grad, axis=0))


def per_device(
    question_states,
    question_ids,
    q_inner_weight,
    q_outer_weight,
    q_norm_gain,
    sql_states,
    sql_ids,
    s_inner_weight,
    s_outer_weight,
    s_norm_gain,
    positive_column,
):
    scale = 1.0 / math.sqrt(D)
    q_place = lax.axis_index("sa")
    s_place = lax.axis_index("pb")
    q_tokens = lax.all_gather(question_states, "sa", axis=1, tiled=True)[0]
    s_tokens = lax.all_gather(sql_states, "pb", axis=1, tiled=True)[0]
    q_rows = q_tokens.shape[0]
    s_rows = s_tokens.shape[0]
    q_hat, q_normed, q_pre, q_weights, q_pooled, q_resid = tower_forward(
        q_tokens, question_ids[0], q_inner_weight, q_norm_gain, False
    )
    s_hat, s_normed, s_pre, s_weights, s_pooled, s_resid = tower_forward(
        s_tokens, sql_ids[0], s_inner_weight, s_norm_gain, True
    )
    q_outer_f = q_outer_weight.astype(jnp.float32)
    s_outer_f = s_outer_weight.astype(jnp.float32)
    q_block = lax.psum(jnp.dot(q_pooled, q_outer_f, precision=HIGH), "sa") + q_resid
    s_block = lax.psum(jnp.dot(s_pooled, s_outer_f, precision=HIGH), "pb") + s_resid
    q_embed = lax.all_gather(q_block, "pb", axis=0, tiled=True)
    s_embed = lax.all_gather(s_block, "sa", axis=0, tiled=True)
    q_pooled_all = lax.all_gather(q_pooled, "pb", axis=0, tiled=True)
    s_pooled_all = lax.all_gather(s_pooled, "sa", axis=0, tiled=True)
    positive_all = lax.all_gather(positive_column, "pb", axis=0, tiled=True)
    score = scale * lax.dot_general(q_embed, s_embed, (((1,), (1,)), ((), ())), precision=HIGH)
    count = score.shape[0]
    match = (positive_all[:, None] == jnp.arange(count, dtype=jnp.int32)[None, :]).astype(
        jnp.float32
    )
    row_max = jnp.max(score, axis=1)
    row_lse = row_max + jnp.log(jnp.sum(jnp.exp(score - row_max[:, None]), axis=1))
    col_max = jnp.max(score, axis=0)
    col_lse = col_max + jnp.log(jnp.sum(jnp.exp(score - col_max[None, :]), axis=0))
    row_pos = jnp.sum(match * score, axis=1)
    col_pos = jnp.sum(match * score, axis=0)
    loss = (jnp.sum(row_lse - row_pos) + jnp.sum(col_lse - col_pos)) / (2.0 * count)
    dscore = 0.5 * (
        jnp.exp(score - row_lse[:, None]) + jnp.exp(score - col_lse[None, :]) - 2.0 * match
    )
    q_grad = scale * jnp.dot(dscore, s_embed, precision=HIGH)
    s_grad = scale * lax.dot_general(dscore, q_embed, (((0,), (0,)), ((), ())), precision=HIGH)
    q_outer_grad = lax.dot_general(q_pooled_all, q_grad, (((0,), (0,)), ((), ())), precision=HIGH)
    s_outer_grad = lax.dot_general(s_pooled_all, s_grad, (((0,), (0,)), ((), ())), precision=HIGH)
    q_grad_own = lax.dynamic_slice_in_dim(q_grad, s_place * q_rows, q_rows, 0)
    s_grad_own = lax.dynamic_slice_in_dim(s_grad, q_place * s_rows, s_rows, 0)
    q_hidden_grad = lax.dot_general(q_grad_own, q_outer_f, (((1,), (1,)), ((), ())), precision=HIGH)
    s_hidden_grad = lax.dot_general(s_grad_own, s_outer_f, (((1,), (1,)), ((), ())), precision=HIGH)
    q_inner_part, q_gain_part = tower_backward(
        q_hat, q_normed, q_pre, q_weights, q_inner_weight, q_hidden_grad
    )
    s_inner_part, s_gain_part = tower_backward(
        s_hat, s_normed, s_pre, s_weights, s_inner_weight, s_hidden_grad
    )
    q_inner_grad = lax.psum(q_inner_part, "pb")
    s_inner_grad = lax.psum(s_inner_part, "sa")
    q_gain_grad, s_gain_grad = lax.psum((q_gain_part, s_gain_part), ("pb", "sa"))
    return (loss, q_inner_grad, q_outer_grad, q_gain_grad, s_inner_grad, s_outer_grad, s_gain_grad)


def solution(mesh):
    placed = (
        P("pb", "sa", None, None),
        P("pb", None, None),
        P(None, "sa"),
        P("sa", None),
        P(),
        P("sa", "pb", None, None),
        P("sa", None, None),
        P(None, "pb"),
        P("pb", None),
        P(),
        P("pb"),
    )
    return jax.shard_map(
        per_device,
        mesh=mesh,
        in_specs=placed,
        out_specs=(P(), P(None, "sa"), P("sa", None), P(), P(None, "pb"), P("pb", None), P()),
        check_vma=False,
    )
```

profile of v0, /device:TPU:25, one launch (start us, length us, event | category | flops | bytes accessed | tf_op | source)
XLA Modules:
  0.0 705.5 jit_solution(16623077752459873952)
XLA Ops:
  14.6 18.9 %all-reduce = s32[256]{0:T(256)} all-reduce(s32[256]{0:T(256)S(1)} %dynamic-update-slice), channel_id=1, replica_groups=mesh['pb'=16,'sa'=16] {'pb'}, use_global_device_ids=true, to_apply=%add | all-reduce | flops 256 | bytes 2048
  33.5 70.1 %all-gather.5.cloned.1.call-done = bf16[1,16,256,768]{3,2,0,1:T(8,128)(2,1)} async-done(((bf16[1,1,256,768]{3,2,0,1:T(8,128)(2,1)}), bf16[1,16,256,768]{3,2,0,1:T(8,128)(2,1)}) %all-gather.5.cloned.1.call-update) | async-done | bytes 6291472 | tf_op jit(solution)/shard_map/all_gather | solution.py:87
  103.6 4.1 multiply_reduce_fusion.2
  107.7 48.2 %all-gather.3.cloned.1.call-done = bf16[1,16,256,768]{3,2,0,1:T(8,128)(2,1)} async-done(((bf16[1,1,256,768]{3,2,0,1:T(8,128)(2,1)}), bf16[1,16,256,768]{3,2,0,1:T(8,128)(2,1)}) %all-gather.3.cloned.1.call-update) | async-done | bytes 6291472 | tf_op jit(solution)/shard_map/all_gather | solution.py:86
  155.9 3.8 convert_reduce_fusion
  164.8 3.8 multiply_multiply_fusion.2
  168.6 2.7 fusion.17
  172.1 69.0 %psum.43 = f32[16,768]{1,0:T(8,128)S(1)} all-reduce(f32[16,768]{1,0:T(8,128)S(1)} %fusion.42), channel_id=1, replica_groups=mesh['pb'=16,'sa'=16] {'pb'}, use_global_device_ids=true, to_apply=%region_6.0 | all-reduce | flops 12288 | bytes 98304 | tf_op jit(solution)/shard_map/psum | solution.py:99
  241.1 5.3 fusion.1
  246.5 32.6 %all_gather.24 = f32[256,768]{1,0:T(8,128)} all-gather(f32[16,768]{1,0:T(8,128)S(1)} %bitcast_add_fusion), channel_id=1, replica_groups=mesh['pb'=16,'sa'=16] {'sa'}, dimensions={0}, use_global_device_ids=true | all-gather | bytes 835584 | tf_op jit(solution)/shard_map/all_gather | solution.py:101
  279.1 4.6 multiply_convert_fusion.1
  289.8 53.6 %psum.42 = f32[16,768]{1,0:T(8,128)S(1)} all-reduce(f32[16,768]{1,0:T(8,128)S(1)} %fusion.41), channel_id=1, replica_groups=mesh['pb'=16,'sa'=16] {'sa'}, use_global_device_ids=true, to_apply=%region_3.0 | all-reduce | flops 12288 | bytes 98304 | tf_op jit(solution)/shard_map/psum | solution.py:98
  343.4 5.4 fusion.3
  348.8 39.3 %all_gather.22 = f32[256,768]{1,0:T(8,128)S(1)} all-gather(f32[16,768]{1,0:T(8,128)S(1)} %bitcast_add_fusion.1), channel_id=1, replica_groups=mesh['pb'=16,'sa'=16] {'pb'}, dimensions={0}, use_global_device_ids=true | all-gather | bytes 835584 | tf_op jit(solution)/shard_map/all_gather | solution.py:100
  393.6 2.7 copy.41
  402.4 4.4 copy.44
  408.2 3.7 fusion.16
  412.2 4.9 multiply_reduce_fusion.1
  417.2 2.8 multiply_reduce_fusion
  420.0 81.8 %all-reduce.1 = (f32[768]{0:T(1024)}, f32[768]{0:T(1024)}) all-reduce(f32[768]{0:T(1024)S(1)} %multiply_reduce_fusion.1, f32[768]{0:T(1024)S(1)} %multiply_reduce_fusion), channel_id=1, replica_groups=mesh['pb'=16,'sa'=16] {'pb','sa'}, use_global_device_ids=true, to_apply=%region_17.0 | all-reduce | flops 1536 | bytes 12288 | tf_op jit(solution)/shard_map/psum | solution.py:136
  501.8 16.7 %all_gather.27 = f32[256,192]{1,0:T(8,128)S(1)} all-gather(f32[16,192]{1,0:T(8,128)S(1)} %bitcast.132), channel_id=1, replica_groups=mesh['pb'=16,'sa'=16] {'sa'}, dimensions={0}, use_global_device_ids=true | all-gather | bytes 208896 | tf_op jit(solution)/shard_map/all_gather | solution.py:103
  518.5 5.5 fusion.47
  524.1 37.7 %all_gather.26 = f32[256,192]{1,0:T(8,128)S(1)} all-gather(f32[16,192]{1,0:T(8,128)S(1)} %bitcast.133), channel_id=1, replica_groups=mesh['pb'=16,'sa'=16] {'pb'}, dimensions={0}, use_global_device_ids=true | all-gather | bytes 208896 | tf_op jit(solution)/shard_map/all_gather | solution.py:102
  564.9 128.9 %all-reduce.7.cloned.1.call-done = f32[768,192]{0,1:T(8,128)} async-done(((f32[768,192]{0,1:T(8,128)}), f32[768,192]{0,1:T(8,128)}) %all-reduce.7.cloned.1.call-update) | async-done | bytes 589840 | tf_op jit(solution)/shard_map/psum | solution.py:135
  (130 shorter events, 37.4 us)
Async XLA Ops:
  7.2 276.5 %copy-start = (bf16[768,192]{0,1:T(8,128)(2,1)S(1)}, bf16[768,192]{0,1:T(8,128)(2,1)}, u32[]{:S(2)}) copy-start(bf16[768,192]{0,1:T(8,128)(2,1)} %param.13) | copy-start | bytes 884740
  7.2 96.4 %all-gather.5.cloned.1.call-start = ((), (), s32[]{:S(2)}) async-start(), calls=%async_computation.1 | async-start | bytes 6684672 | tf_op jit(solution)/shard_map/all_gather | solution.py:87
  7.9 148.0 %all-gather.3.cloned.1.call-start = ((), (), s32[]{:S(2)}) async-start(), calls=%async_computation | async-start | bytes 6684672 | tf_op jit(solution)/shard_map/all_gather | solution.py:86
  8.7 556.3 %all-reduce.5.cloned.1.call-start = ((), (), s32[]{:S(2)}) async-start(), calls=%async_computation.2 | async-start | bytes 1179648 | tf_op jit(solution)/shard_map/psum | solution.py:134
  107.7 54.8 %copy-start.19 = (f32[2,2,8,128]{3,1,2,0:T(2,128)}, f32[2,2,8,128]{3,1,2,0:T(2,128)S(1)}, u32[]{:S(2)}) copy-start(f32[2,2,8,128]{3,1,2,0:T(2,128)S(1)} %copy.38) | copy-start | bytes 49156
  159.8 119.3 %copy-start.21 = (f32[2,2,8,128]{3,1,2,0:T(2,128)}, f32[2,2,8,128]{3,1,2,0:T(2,128)S(1)}, u32[]{:S(2)}) copy-start(f32[2,2,8,128]{3,1,2,0:T(2,128)S(1)} %copy.36) | copy-start | bytes 49156
  162.5 116.6 %copy-start.23 = (f32[2,2,8,128]{3,1,2,0:T(2,128)}, f32[2,2,8,128]{3,1,2,0:T(2,128)S(1)}, u32[]{:S(2)}) copy-start(f32[2,2,8,128]{3,1,2,0:T(2,128)S(1)} %copy.37) | copy-start | bytes 49156
  241.1 38.0 %copy-start.29 = (f32[768]{0:T(1024)S(1)}, f32[768]{0:T(1024)}, u32[]{:S(2)}) copy-start(f32[768]{0:T(1024)} %param.15) | copy-start | bytes 9220
  343.3 44.7 %copy-start.5 = (f32[256,768]{1,0:T(8,128)S(1)}, f32[256,768]{1,0:T(8,128)}, u32[]{:S(2)}) copy-start(f32[256,768]{1,0:T(8,128)} %all_gather.24) | copy-start | bytes 2359300
  343.4 45.7 %copy-start.27 = (s32[256]{0:T(256)S(1)}, s32[256]{0:T(256)}, u32[]{:S(2)}) copy-start(s32[256]{0:T(256)} %all-reduce) | copy-start | bytes 3076
  348.8 43.9 %copy-start.12 = (bf16[192,768]{1,0:T(8,128)(2,1)S(1)}, bf16[192,768]{1,0:T(8,128)(2,1)}, u32[]{:S(2)}) copy-start(bf16[192,768]{1,0:T(8,128)(2,1)} %param.14) | copy-start | bytes 884740
  393.6 5.4 slice-start.4
  401.3 292.6 %all-reduce.7.cloned.1.call-start = ((), (), s32[]{:S(2)}) async-start(), calls=%async_computation.3 | async-start | bytes 1179648 | tf_op jit(solution)/shard_map/psum | solution.py:135
  402.4 5.8 copy-start.17
  402.4 9.5 %slice-start = ((s8[6291456]{0:T(1024)(128)(4,1)}), s8[2097152]{0:T(1024)(128)(4,1)S(1)}, s32[]{:S(2)}) async-start(s8[6291456]{0:T(1024)(128)(4,1)} %bitcast.112), calls=%async_computation.4 | async-start | bytes 4194304
  402.4 9.5 %copy-start.22 = (f32[2,2,8,128]{3,1,2,0:T(2,128)S(1)}, f32[2,2,8,128]{3,1,2,0:T(2,128)}, u32[]{:S(2)}) copy-start(f32[2,2,8,128]{3,1,2,0:T(2,128)} %copy-done.21) | copy-start | bytes 49156
  402.4 9.5 %copy-start.24 = (f32[2,2,8,128]{3,1,2,0:T(2,128)S(1)}, f32[2,2,8,128]{3,1,2,0:T(2,128)}, u32[]{:S(2)}) copy-start(f32[2,2,8,128]{3,1,2,0:T(2,128)} %copy-done.23) | copy-start | bytes 49156
  408.2 9.0 %slice-start.2 = ((s8[6291456]{0:T(1024)(128)(4,1)}), s8[4194304]{0:T(1024)(128)(4,1)S(1)}, s32[]{:S(2)}) async-start(s8[6291456]{0:T(1024)(128)(4,1)} %bitcast.114), calls=%async_computation.6 | async-start | bytes 8388608
  412.2 5.0 slice-start.3
  412.2 5.0 copy-start.16
  412.2 5.0 copy-start.20
  417.2 84.6 %copy-start.25 = (f32[16,1,192]{2,0,1:T(8,128)S(1)}, f32[16,1,192]{2,0,1:T(8,128)}, u32[]{:S(2)}) copy-start(f32[16,1,192]{2,0,1:T(8,128)} %copy.67) | copy-start | bytes 36868
  518.5 5.6 copy-start.26
  518.5 44.9 %copy-start.7 = (f32[256,768]{1,0:T(8,128)S(1)}, f32[256,768]{1,0:T(8,128)}, u32[]{:S(2)}) copy-start(f32[256,768]{1,0:T(8,128)} %copy-done.6) | copy-start | bytes 2359300
  (16 other events, 47.3 us)
Sparse Core Ops, SparseCore 0:
  10.5 93.0 all-gather.4
  105.5 50.4 all-gather.2
  401.4 159.6 all-reduce.4
  564.3 129.4 all-reduce.6
where the time goes:
time: 713 us; the launch traced here: 706 us
  blocking collectives  350 us (49%)
  waiting for transfers between devices  249 us (35%)
  matrix products  45.8 us (6%)
  other arithmetic  25 us (4%)
  local copies, waits for them, and re-layouts  18.6 us (3%)
  between operations  17.6 us (2%)
    psum x1, waiting for transfers between devices, per_device(): s_inner_grad = lax.psum(s_inner_part, 'sa')  129 us
    psum x1, blocking collectives, per_device(): lax.psum((q_gain_part, s_gain_part), ('pb', 'sa'))  81.8 us
    all_gather x1, waiting for transfers between devices, per_device(): s_tokens = lax.all_gather(sql_states, 'pb', axis=1, tiled=True)[0]  70.1 us
    psum x1, blocking collectives, per_device(): lax.psum(jnp.dot(s_pooled, s_outer_f, precision=HIGH), 'pb') + s_resid  69 us
    psum x1, blocking collectives, per_device(): lax.psum(jnp.dot(q_pooled, q_outer_f, precision=HIGH), 'sa') + q_resid  53.6 us
    all_gather x1, waiting for transfers between devices, per_device(): q_tokens = lax.all_gather(question_states, 'sa', axis=1, tiled=True)[0]  48.2 us
    all_gather x1, blocking collectives, per_device(): q_embed = lax.all_gather(q_block, 'pb', axis=0, tiled=True)  39.3 us
    all_gather x1, blocking collectives, per_device(): q_pooled_all = lax.all_gather(q_pooled, 'pb', axis=0, tiled=True)  37.7 us
  transfers between devices with their start and end apart: 4, of which 3 were waited for; matrix products, arithmetic and copies ran while one was open for 5% of the time, Pallas kernels for 0%

commit v1 on v0

--- a/solution.py
+++ b/solution.py
@@ -132,7 +132,7 @@
         s_hat, s_normed, s_pre, s_weights, s_inner_weight, s_hidden_grad
     )
     q_inner_grad = lax.psum(q_inner_part, "pb")
-    s_inner_grad = lax.psum(s_inner_part, "sa")
+    s_inner_grad = jnp.sum(lax.all_gather(s_inner_part, "sa"), axis=0)
     q_gain_grad, s_gain_grad = lax.psum((q_gain_part, s_gain_part), ("pb", "sa"))
     return (loss, q_inner_grad, q_outer_grad, q_gain_grad, s_inner_grad, s_outer_grad, s_gain_grad)
 

time: 713 us -> 666 us (0.934)
  the two profiles are of different devices: /device:TPU:25 before, /device:TPU:24 now
where the time goes in v1:
time: 666 us; the launch traced here: 658 us
  blocking collectives  361 us (54%)
  waiting for transfers between devices  185 us (28%)
  matrix products  43.9 us (7%)
  other arithmetic  25.8 us (4%)
  local copies, waits for them, and re-layouts  24.4 us (4%)
  between operations  18 us (3%)
    psum x1, blocking collectives, per_device(): lax.psum(jnp.dot(s_pooled, s_outer_f, precision=HIGH), 'pb') + s_resid  82.6 us
    psum x1, blocking collectives, per_device(): lax.psum((q_gain_part, s_gain_part), ('pb', 'sa'))  75.1 us
    psum x1, waiting for transfers between devices, per_device(): q_inner_grad = lax.psum(q_inner_part, 'pb')  68.9 us
    all_gather x1, waiting for transfers between devices, per_device(): s_tokens = lax.all_gather(sql_states, 'pb', axis=1, tiled=True)[0]  66.5 us
    psum x1, blocking collectives, per_device(): lax.psum(jnp.dot(q_pooled, q_outer_f, precision=HIGH), 'sa') + q_resid  51.7 us
    all_gather x1, waiting for transfers between devices, per_device(): q_tokens = lax.all_gather(question_states, 'sa', axis=1, tiled=True)[0]  47.8 us
    all_gather x1, blocking collectives, per_device(): q_embed = lax.all_gather(q_block, 'pb', axis=0, tiled=True)  44.6 us
    all_gather x1, blocking collectives, per_device(): q_pooled_all = lax.all_gather(q_pooled, 'pb', axis=0, tiled=True)  44 us
  transfers between devices with their start and end apart: 4, of which 3 were waited for; matrix products, arithmetic and copies ran while one was open for 6% of the time, Pallas kernels for 0%

profile of v1, /device:TPU:24, one launch (start us, length us, event | category | flops | bytes accessed | tf_op | source)
XLA Modules:
  0.0 658.1 jit_solution(12501537187548569675)
XLA Ops:
  13.1 21.9 %all-reduce = s32[256]{0:T(256)} all-reduce(s32[256]{0:T(256)S(1)} %dynamic-update-slice), channel_id=1, replica_groups=mesh['pb'=16,'sa'=16] {'pb'}, use_global_device_ids=true, to_apply=%add | all-reduce | flops 256 | bytes 2048
  37.1 66.5 %all-gather.7.cloned.1.call-done = bf16[1,16,256,768]{3,2,0,1:T(8,128)(2,1)} async-done(((bf16[1,1,256,768]{3,2,0,1:T(8,128)(2,1)}), bf16[1,16,256,768]{3,2,0,1:T(8,128)(2,1)}) %all-gather.7.cloned.1.call-update) | async-done | bytes 6291472 | tf_op jit(solution)/shard_map/all_gather | solution.py:87
  103.6 4.1 multiply_reduce_fusion.2
  107.7 47.8 %all-gather.5.cloned.1.call-done = bf16[1,16,256,768]{3,2,0,1:T(8,128)(2,1)} async-done(((bf16[1,1,256,768]{3,2,0,1:T(8,128)(2,1)}), bf16[1,16,256,768]{3,2,0,1:T(8,128)(2,1)}) %all-gather.5.cloned.1.call-update) | async-done | bytes 6291472 | tf_op jit(solution)/shard_map/all_gather | solution.py:86
  155.5 3.8 convert_reduce_fusion
  164.4 3.6 multiply_multiply_fusion.2
  168.0 2.7 fusion.17
  171.0 82.6 %psum.36 = f32[16,768]{1,0:T(8,128)S(1)} all-reduce(f32[16,768]{1,0:T(8,128)S(1)} %fusion.42), channel_id=1, replica_groups=mesh['pb'=16,'sa'=16] {'pb'}, use_global_device_ids=true, to_apply=%region_6.0 | all-reduce | flops 12288 | bytes 98304 | tf_op jit(solution)/shard_map/psum | solution.py:99
  253.5 5.3 fusion.1
  258.9 18.6 %all_gather.30 = f32[256,768]{1,0:T(8,128)} all-gather(f32[16,768]{1,0:T(8,128)S(1)} %bitcast_add_fusion), channel_id=1, replica_groups=mesh['pb'=16,'sa'=16] {'sa'}, dimensions={0}, use_global_device_ids=true | all-gather | bytes 835584 | tf_op jit(solution)/shard_map/all_gather | solution.py:101
  277.5 4.6 multiply_convert_fusion.1
  284.8 2.7 fusion.20
  288.3 51.7 %psum.35 = f32[16,768]{1,0:T(8,128)S(1)} all-reduce(f32[16,768]{1,0:T(8,128)S(1)} %fusion.41), channel_id=1, replica_groups=mesh['pb'=16,'sa'=16] {'sa'}, use_global_device_ids=true, to_apply=%region_3.0 | all-reduce | flops 12288 | bytes 98304 | tf_op jit(solution)/shard_map/psum | solution.py:98
  340.0 5.4 fusion.3
  345.4 44.6 %all_gather.28 = f32[256,768]{1,0:T(8,128)S(1)} all-gather(f32[16,768]{1,0:T(8,128)S(1)} %bitcast_add_fusion.1), channel_id=1, replica_groups=mesh['pb'=16,'sa'=16] {'pb'}, dimensions={0}, use_global_device_ids=true | all-gather | bytes 835584 | tf_op jit(solution)/shard_map/all_gather | solution.py:100
  394.6 2.8 copy.44
  407.7 2.7 copy.41
  410.4 22.6 %all_gather.35 = f32[256,192]{1,0:T(8,128)S(1)} all-gather(f32[16,192]{1,0:T(8,128)S(1)} %bitcast.139), channel_id=1, replica_groups=mesh['pb'=16,'sa'=16] {'sa'}, dimensions={0}, use_global_device_ids=true | all-gather | bytes 208896 | tf_op jit(solution)/shard_map/all_gather | solution.py:103
  433.0 44.0 %all_gather.32 = f32[256,192]{1,0:T(8,128)} all-gather(f32[16,192]{1,0:T(8,128)S(1)} %bitcast.140), channel_id=1, replica_groups=mesh['pb'=16,'sa'=16] {'pb'}, dimensions={0}, use_global_device_ids=true | all-gather | bytes 208896 | tf_op jit(solution)/shard_map/all_gather | solution.py:102
  483.5 5.2 multiply_reduce_fusion.1
  488.8 2.6 multiply_reduce_fusion
  494.3 75.1 %all-reduce.1 = (f32[768]{0:T(1024)}, f32[768]{0:T(1024)}) all-reduce(f32[768]{0:T(1024)S(1)} %multiply_reduce_fusion.1, f32[768]{0:T(1024)S(1)} %multiply_reduce_fusion), channel_id=1, replica_groups=mesh['pb'=16,'sa'=16] {'pb','sa'}, use_global_device_ids=true, to_apply=%region_17.0 | all-reduce | flops 1536 | bytes 12288 | tf_op jit(solution)/shard_map/psum | solution.py:136
  569.4 7.2 %copy.45 = f32[24,8,16,768]{3,2,1,0:T(8,128)S(1)} copy(f32[24,8,16,768]{3,1,2,0:T(8,128)} %bitcast.129) | data formatting | bytes 18874368
  579.1 68.9 %all-reduce.4.cloned.1.call-done = f32[768,192]{0,1:T(8,128)} async-done(((f32[768,192]{0,1:T(8,128)}), f32[768,192]{0,1:T(8,128)}) %all-reduce.4.cloned.1.call-update) | async-done | bytes 589840 | tf_op jit(solution)/shard_map/psum | solution.py:134
  (145 shorter events, 43.0 us)
Async XLA Ops:
  7.2 274.9 %copy-start = (bf16[768,192]{0,1:T(8,128)(2,1)S(1)}, bf16[768,192]{0,1:T(8,128)(2,1)}, u32[]{:S(2)}) copy-start(bf16[768,192]{0,1:T(8,128)(2,1)} %param.13) | copy-start | bytes 884740
  7.2 96.4 %all-gather.7.cloned.1.call-start = ((), (), s32[]{:S(2)}) async-start(), calls=%async_computation.1 | async-start | bytes 6684672 | tf_op jit(solution)/shard_map/all_gather | solution.py:87
  7.9 147.6 %all-gather.5.cloned.1.call-start = ((), (), s32[]{:S(2)}) async-start(), calls=%async_computation | async-start | bytes 6684672 | tf_op jit(solution)/shard_map/all_gather | solution.py:86
  8.7 560.7 %all-gather.9.cloned.1.call-start = ((), (), s32[]{:S(2)}) async-start(), calls=%async_computation.3 | async-start | bytes 10027008 | tf_op jit(solution)/shard_map/all_gather | solution.py:135
  107.7 54.4 %copy-start.26 = (f32[2,2,8,128]{3,1,2,0:T(2,128)}, f32[2,2,8,128]{3,1,2,0:T(2,128)S(1)}, u32[]{:S(2)}) copy-start(f32[2,2,8,128]{3,1,2,0:T(2,128)S(1)} %copy.38) | copy-start | bytes 49156
  155.5 4.6 copy-start.1
  159.4 118.1 %copy-start.28 = (f32[2,2,8,128]{3,1,2,0:T(2,128)}, f32[2,2,8,128]{3,1,2,0:T(2,128)S(1)}, u32[]{:S(2)}) copy-start(f32[2,2,8,128]{3,1,2,0:T(2,128)S(1)} %copy.36) | copy-start | bytes 49156
  162.1 115.4 %copy-start.30 = (f32[2,2,8,128]{3,1,2,0:T(2,128)}, f32[2,2,8,128]{3,1,2,0:T(2,128)S(1)}, u32[]{:S(2)}) copy-start(f32[2,2,8,128]{3,1,2,0:T(2,128)S(1)} %copy.37) | copy-start | bytes 49156
  164.4 3.6 copy-start.4
  170.7 88.2 %copy-start.21 = (f32[16,1,192]{2,1,0:T(1,128)}, f32[16,1,192]{2,1,0:T(1,128)S(1)}, u32[]{:S(2)}) copy-start(f32[16,1,192]{2,1,0:T(1,128)S(1)} %fusion.17) | copy-start | bytes 36868
  253.5 24.0 %copy-start.36 = (f32[768]{0:T(1024)S(1)}, f32[768]{0:T(1024)}, u32[]{:S(2)}) copy-start(f32[768]{0:T(1024)} %param.15) | copy-start | bytes 9220
  340.0 50.0 %copy-start.6 = (f32[256,768]{1,0:T(8,128)S(1)}, f32[256,768]{1,0:T(8,128)}, u32[]{:S(2)}) copy-start(f32[256,768]{1,0:T(8,128)} %all_gather.30) | copy-start | bytes 2359300
  340.0 50.9 %copy-start.34 = (s32[256]{0:T(256)S(1)}, s32[256]{0:T(256)}, u32[]{:S(2)}) copy-start(s32[256]{0:T(256)} %all-reduce) | copy-start | bytes 3076
  345.4 48.3 %copy-start.16 = (bf16[192,768]{1,0:T(8,128)(2,1)S(1)}, bf16[192,768]{1,0:T(8,128)(2,1)}, u32[]{:S(2)}) copy-start(bf16[192,768]{1,0:T(8,128)(2,1)} %param.19) | copy-start | bytes 884740
  394.6 5.5 slice-start.4
  402.4 245.6 %all-reduce.4.cloned.1.call-start = ((), (), s32[]{:S(2)}) async-start(), calls=%async_computation.2 | async-start | bytes 1179648 | tf_op jit(solution)/shard_map/psum | solution.py:134
  407.6 69.4 %copy-start.9 = (f32[256,768]{1,0:T(8,128)S(1)}, f32[256,768]{1,0:T(8,128)}, u32[]{:S(2)}) copy-start(f32[256,768]{1,0:T(8,128)} %copy-done.8) | copy-start | bytes 2359300
  407.6 73.5 %slice-start.2 = ((s8[6291456]{0:T(1024)(128)(4,1)}), s8[2097152]{0:T(1024)(128)(4,1)S(1)}, s32[]{:S(2)}) async-start(s8[6291456]{0:T(1024)(128)(4,1)} %bitcast.119), calls=%async_computation.6 | async-start | bytes 4194304
  477.0 4.1 slice-start.3
  481.1 7.6 %slice-start = ((s8[6291456]{0:T(1024)(128)(4,1)}), s8[2097152]{0:T(1024)(128)(4,1)S(1)}, s32[]{:S(2)}) async-start(s8[6291456]{0:T(1024)(128)(4,1)} %bitcast.117), calls=%async_computation.4 | async-start | bytes 4194304
  483.4 5.3 slice-start.1
  483.5 5.3 copy-start.13
  483.5 5.3 copy-start.20
  483.5 5.3 copy-start.27
  (23 other events, 51.2 us)
Sparse Core Ops, SparseCore 0:
  10.5 93.0 all-gather.6
  105.5 50.0 all-gather.4
  402.5 63.6 all-gather.8
  483.5 164.3 all-reduce.3
